TPU v7x, 32 devices: a whole 2x2x4 slice. The times are simulated.
32 devices in a mesh: island: 2 (over core), dp: 4 (over z), tensor: 4 (over y, x).
Axes of the slice: x: 2, y: 2, z: 4, core: 2. Of those that a mesh axis runs over, the one named last changes fastest.
Arguments:
- pseudo_grad: float32 [2, 48, 256, 5120], P('island', None, 'dp', 'tensor'), may hold values from -1000 to 1000, as said below
- block_owner: int32 [48], replicated, may hold values from 0 to 7, as said below
Outputs:
- update: bfloat16 [8, 12, 256, 5120], P(('island', 'dp'), None, None, 'tensor')
Inputs may be any that keep to these rules, and one draw needn't show every extreme that they name: `pseudo_grad`: float pseudo-gradients; entries lie within the range. `block_owner`: every owner holds at most 12 blocks and at least one; some owner holds exactly 12.
All inputs are finite; a program needn't handle non-finite values.
Results may differ from a plain program's by a relative error of at most 0.001.
Values sent between devices are 32-bit elements; how exact they have to be, the bound alone decides.
A program may use at most 128 MiB of HBM per device.

v0:
```python
import math
import jax
import jax.numpy as jnp
from jax import lax
from jax.sharding import PartitionSpec as P

D = 5120
COEF_A = 3.4445
COEF_B = -4.775
COEF_C = 2.0315
EPSILON = 1e-07


def slot_table(block_owner, owner_count, slot_count):
    blocks = block_owner.shape[0]
    positions = jnp.arange(blocks, dtype=jnp.int32)
    one_hot = (block_owner[:, None] == jnp.arange(owner_count, dtype=jnp.int32)[None, :]).astype(
        jnp.float32
    )
    earlier = (positions[None, :] < positions[:, None]).astype(jnp.float32)
    counts_before = jnp.dot(earlier, one_hot, precision=lax.Precision.HIGHEST)
    slot = jnp.sum(counts_before * one_hot, axis=1).astype(jnp.int32)
    slot_key = block_owner * slot_count + slot
    entries = jnp.arange(owner_count * slot_count, dtype=jnp.int32)
    matches = slot_key[None, :] == entries[:, None]
    slot_index = jnp.sum(jnp.where(matches, positions[None, :], 0), axis=1)
    slot_valid = jnp.any(matches, axis=1)
    return (slot_index, slot_valid)


def batch_dot(left, right):
    return jnp.einsum("khg,kgc->khc", left, right, precision=lax.Precision.HIGHEST)


def polynomial(gram_mat):
    return COEF_B * gram_mat + COEF_C * batch_dot(gram_mat, gram_mat)


def orthogonalize(incoming):
    blocks = incoming[0]
    partial_value = jnp.einsum("khc,kgc->khg", blocks, blocks, precision=lax.Precision.HIGHEST)
    gram_first = lax.psum(partial_value, "tensor")
    squares = jnp.trace(gram_first, axis1=1, axis2=2)
    inverse = 1.0 / (jnp.sqrt(squares) + EPSILON)
    start = blocks * inverse[:, None, None]
    gram_start = gram_first * (inverse * inverse)[:, None, None]
    poly_first = polynomial(gram_start)
    identity = jnp.eye(blocks.shape[1], dtype=jnp.float32)[None]
    first_factor = COEF_A * identity + poly_first
    gram_second = batch_dot(batch_dot(first_factor, gram_start), first_factor)
    second_factor = COEF_A * identity + polynomial(gram_second)
    final = batch_dot(batch_dot(second_factor, first_factor), start)
    return (math.sqrt(D) * final).astype(jnp.bfloat16)[None]


def body(pseudo_grad, block_owner):
    own_grad = pseudo_grad[0]
    blocks = block_owner.shape[0]
    dp_count = lax.axis_size("dp")
    island_count = lax.axis_size("island")
    owner_count = island_count * dp_count
    slot_count = 2 * (blocks // owner_count)
    row_count = own_grad.shape[1]
    col_count = own_grad.shape[2]
    slot_index, slot_valid = slot_table(block_owner, owner_count, slot_count)
    summed = lax.psum(own_grad, "island")
    island = lax.axis_index("island")
    own_index = lax.dynamic_slice_in_dim(
        slot_index, island * dp_count * slot_count, dp_count * slot_count
    )
    own_valid = lax.dynamic_slice_in_dim(
        slot_valid, island * dp_count * slot_count, dp_count * slot_count
    )
    picked = jnp.take(summed, own_index, axis=0)
    picked = jnp.where(own_valid[:, None, None], picked, 0.0)
    outgoing = picked.reshape(dp_count, slot_count, row_count, col_count)
    return orthogonalize(lax.all_to_all(outgoing, "dp", split_axis=0, concat_axis=2, tiled=True))


def solution(mesh):
    in_specs = (P("island", None, "dp", "tensor"), P())
    out_specs = P(("island", "dp"), None, None, "tensor")
    return jax.shard_map(body, mesh=mesh, in_specs=in_specs, out_specs=out_specs, check_vma=False)
```

profile of v0, /device:TPU:0, one launch (start us, length us, event | category | flops | bytes accessed | tf_op | source)
XLA Modules:
  0.0 606.4 jit_solution(15884312456623883124)
XLA Ops:
  6.5 0.7 all-reduce.3.cloned.1.call-update
  7.3 0.0 all-reduce.5.cloned.1.call-start
  7.3 0.1 fusion.36
  7.5 0.1 select_reduce_fusion.1
  7.6 0.1 compare_and_fusion
  7.7 0.1 broadcast_in_dim.67
  7.7 0.1 fusion.37
  7.8 0.1 dynamic_slice.6
  7.9 0.1 broadcast_in_dim.63
  8.0 60.4 %all-reduce.3.cloned.1.call-done = f32[48,64,1280]{2,1,0:T(8,128)} async-done(((f32[48,64,1280]{2,1,0:T(8,128)}), f32[48,64,1280]{2,1,0:T(8,128)}) %all-reduce.3.cloned.1.call-update) | async-done | bytes 15728656 | tf_op jit(solution)/shard_map/psum | solution.py:66
  68.4 14.6 %gather_fusion = f32[48,64,1280]{2,1,0:T(8,128)} fusion(f32[48,64,1280]{2,1,0:T(8,128)} %all-reduce.3.cloned.1.call-done, s32[1024]{0:T(1024)S(1)} %pad_clamp_fusion), kind=kCustom, calls=%fused_computation | custom fusion | bytes 31457472 | tf_op jit(solution)/shard_map/jit(_take)/gather | solution.py:74
  83.0 6.7 %select_select_fusion = f32[4,12,64,1280]{3,2,1,0:T(8,128)S(1)} fusion(f32[4,12,64,1280]{3,2,1,0:T(8,128)} %bitcast.16, pred[4,12]{1,0:T(4,128)(4,1)S(1)} %broadcast_in_dim.67, pred[4,12]{1,0:T(4,128)(4,1)S(1)} %broadcast_in_dim.63), kind=kLoop, calls=%fused_computation.4 | loop fusion | flops 7864320 | bytes 31457376 | tf_op jit(solution)/shard_map/jit(_where)/select_n | solution.py:75
  89.6 345.5 %all_to_all.15 = f32[4,12,64,1280]{3,2,1,0:T(8,128)} all-to-all(f32[4,12,64,1280]{3,2,1,0:T(8,128)S(1)} %select_select_fusion), channel_id=1, replica_groups=mesh['island'=2,'dp'=4,'tensor'=4] {'dp'}, dimensions={0} | all-to-all | bytes 31457280 | tf_op jit(solution)/shard_map/all_to_all | solution.py:77
  435.1 12.7 %copy.7 = f32[1,12,4,64,1280]{4,3,2,1,0:T(8,128)} copy(f32[1,12,4,64,1280]{4,3,1,2,0:T(8,128)} %bitcast.17) | data formatting | bytes 31457280 | tf_op jit(solution)/shard_map/all_to_all | solution.py:77
  447.9 21.9 %fusion.46 = f32[12,256,256]{2,1,0:T(8,128)} fusion(f32[12,256,1280]{2,1,0:T(8,128)} %bitcast.14), kind=kOutput, calls=%fused_computation.59 | convolution fusion | flops 12079595520 | bytes 18874368 | tf_op jit(solution)/shard_map/khc,kgc->khg/dot_general | solution.py:41
  469.9 86.2 %all-reduce.5.cloned.1.call-done = f32[12,256,256]{2,1,0:T(8,128)} async-done(((f32[12,256,256]{2,1,0:T(8,128)}), f32[12,256,256]{2,1,0:T(8,128)}) %all-reduce.5.cloned.1.call-update) | async-done | bytes 3145744 | tf_op jit(solution)/shard_map/psum | solution.py:42
  556.1 2.5 select_reduce_fusion
  558.6 0.3 copy-done
  558.9 3.4 fusion.20
  562.4 4.1 fusion.14
  566.5 3.8 fusion.13
  570.4 3.7 fusion.47
  574.1 4.5 fusion.8
  578.6 20.8 %fusion.5 = bf16[1,12,256,1280]{3,2,1,0:T(8,128)(2,1)} fusion(f32[12,256,256]{2,1,0:T(8,128)S(1)} %fusion.8, f32[12,256,1280]{2,1,0:T(8,128)} %bitcast.15, f32[12]{0:T(128)S(1)} %get-tuple-element.6), kind=kOutput, calls=%fused_computation.6 | convolution fusion | flops 12091392000 | bytes 26738736 | tf_op jit(solution)/shard_map/khg,kgc->khc/dot_general | solution.py:32
  (10 shorter events, 0.1 us)
Async XLA Ops:
  6.5 61.9 %all-reduce.3.cloned.1.call-start = ((), (), s32[]{:S(2)}) async-start(), calls=%async_computation.1 | async-start | bytes 31457280 | tf_op jit(solution)/shard_map/psum | solution.py:66
  6.5 0.8 copy-start.1
  7.3 548.8 %all-reduce.5.cloned.1.call-start = ((), (), s32[]{:S(2)}) async-start(), calls=%async_computation.2 | async-start | bytes 6291456 | tf_op jit(solution)/shard_map/psum | solution.py:42
  556.1 2.8 copy-start
Sparse Core Ops, SparseCore 0:
  9.8 58.5 all-reduce.2
  470.0 86.0 all-reduce.4
where the time goes:
time: 613 us; the launch traced here: 606 us
  blocking collectives  346 us (56%)
  waiting for transfers between devices  147 us (24%)
  matrix products  62.5 us (10%)
  local copies, waits for them, and re-layouts  27.9 us (5%)
  between operations  13.7 us (2%)
  other arithmetic  9.49 us (2%)
    all_to_all x1, blocking collectives, body(): lax.all_to_all(outgoing, 'dp', split_axis=0, concat_axis=2, tiled=True)  346 us
    psum x1, waiting for transfers between devices, orthogonalize(): gram_first = lax.psum(partial_value, 'tensor')  86.2 us
    psum x1, waiting for transfers between devices, body(): summed = lax.psum(own_grad, 'island')  60.4 us
    dot_general x6, matrix products, batch_dot(): jnp.einsum('khg,kgc->khc', left, right, precision=lax.Precision.HIGHEST)  40.4 us
    dot_general x1, matrix products, orthogonalize(): jnp.einsum('khc,kgc->khg', blocks, blocks, precision=lax.Precision.HIGHEST)  21.9 us
    gather x1, local copies, waits for them, and re-layouts, body(): picked = jnp.take(summed, own_index, axis=0)  14.6 us
    all_to_all x1, local copies, waits for them, and re-layouts, body(): lax.all_to_all(outgoing, 'dp', split_axis=0, concat_axis=2, tiled=True)  12.7 us
  transfers between devices with their start and end apart: 2, of which 2 were waited for; matrix products, arithmetic and copies ran while one was open for 0% of the time, Pallas kernels for 0%

commit v1 on v0

--- a/solution.py
+++ b/solution.py
@@ -74,7 +74,12 @@
     picked = jnp.take(summed, own_index, axis=0)
     picked = jnp.where(own_valid[:, None, None], picked, 0.0)
     outgoing = picked.reshape(dp_count, slot_count, row_count, col_count)
-    return orthogonalize(lax.all_to_all(outgoing, "dp", split_axis=0, concat_axis=2, tiled=True))
+    return orthogonalize(
+        jnp.concatenate(
+            lax.all_to_all(jnp.stack(jnp.split(outgoing, lax.axis_size("dp"), axis=0)), "dp", 0, 0),
+            axis=2,
+        )
+    )
 
 
 def solution(mesh):

time: 613 us -> 636 us (1.038)
  local copies, waits for them, and re-layouts: 27.9 us -> 39.3 us
  other arithmetic: 9.49 us -> 20.6 us
    reshape x0 -> x1, local copies, waits for them, and re-layouts: none -> 12.7 us  [body(): jnp.concatenate(lax.all_to_all(jnp.stack(jnp.split(outgoing, lax.axis_siz...]
    all_to_all x1 -> x0, local copies, waits for them, and re-layouts: 12.7 us -> none  [body(): lax.all_to_all(outgoing, 'dp', split_axis=0, concat_axis=2, tiled=True)]
    another operation x0 -> x1, local copies, waits for them, and re-layouts: none -> 11.6 us  [body(): jnp.stack(jnp.split(outgoing, lax.axis_size('dp'), axis=0))]
where the time goes in v1:
time: 636 us; the launch traced here: 629 us
  blocking collectives  346 us (54%)
  waiting for transfers between devices  147 us (23%)
  matrix products  62.4 us (10%)
  local copies, waits for them, and re-layouts  39.3 us (6%)
  other arithmetic  20.6 us (3%)
  between operations  13.7 us (2%)
    all_to_all x1, blocking collectives, body(): lax.all_to_all(jnp.stack(jnp.split(outgoing, lax.axis_size('dp'), axis=0)...  346 us
    psum x1, waiting for transfers between devices, orthogonalize(): gram_first = lax.psum(partial_value, 'tensor')  86.2 us
    psum x1, waiting for transfers between devices, body(): summed = lax.psum(own_grad, 'island')  60.6 us
    dot_general x6, matrix products, batch_dot(): jnp.einsum('khg,kgc->khc', left, right, precision=lax.Precision.HIGHEST)  40.1 us
    dot_general x1, matrix products, orthogonalize(): jnp.einsum('khc,kgc->khg', blocks, blocks, precision=lax.Precision.HIGHEST)  22.1 us
    gather x1, local copies, waits for them, and re-layouts, body(): picked = jnp.take(summed, own_index, axis=0)  14.6 us
    reshape x1, local copies, waits for them, and re-layouts, body(): jnp.concatenate(lax.all_to_all(jnp.stack(jnp.split(outgoing, lax.axis_siz...  12.7 us
  transfers between devices with their start and end apart: 2, of which 2 were waited for; matrix products, arithmetic and copies ran while one was open for 0% of the time, Pallas kernels for 0%

profile of v1, /device:TPU:0, one launch (start us, length us, event | category | flops | bytes accessed | tf_op | source)
XLA Modules:
  0.0 629.1 jit_solution(16390810250004174804)
XLA Ops:
  6.5 0.7 all-reduce.3.cloned.1.call-update
  7.3 0.0 all-reduce.5.cloned.1.call-start
  7.3 0.1 fusion.36
  7.5 0.1 fusion.37
  7.6 0.1 dynamic_slice.6
  7.6 0.1 select_reduce_fusion.1
  7.7 0.1 compare_and_fusion
  7.8 60.6 %all-reduce.3.cloned.1.call-done = f32[48,64,1280]{2,1,0:T(8,128)} async-done(((f32[48,64,1280]{2,1,0:T(8,128)}), f32[48,64,1280]{2,1,0:T(8,128)}) %all-reduce.3.cloned.1.call-update) | async-done | bytes 15728656 | tf_op jit(solution)/shard_map/psum | solution.py:66
  68.4 14.6 %gather_fusion = f32[48,64,1280]{2,1,0:T(8,128)} fusion(f32[48,64,1280]{2,1,0:T(8,128)} %all-reduce.3.cloned.1.call-done, s32[1024]{0:T(1024)S(1)} %pad_clamp_fusion), kind=kCustom, calls=%fused_computation | custom fusion | bytes 31457472 | tf_op jit(solution)/shard_map/jit(_take)/gather | solution.py:74
  83.0 11.5 %select_select_fusion = f32[48,64,1280]{2,1,0:T(8,128)} fusion(f32[48,64,1280]{2,1,0:T(8,128)} %gather_fusion, pred[48]{0:T(512)(128)(4,1)S(1)} %get-tuple-element.7, pred[48]{0:T(512)(128)(4,1)S(1)} %dynamic_slice.6), kind=kLoop, calls=%fused_computation.5 | loop fusion | flops 7864320 | bytes 31457376 | tf_op jit(solution)/shard_map/jit(_where)/select_n | solution.py:75
  94.5 11.6 %slice_bitcast_fusion.3 = (f32[1,1,12,64,1280]{4,3,2,1,0:T(8,128)}, f32[1,1,12,64,1280]{4,3,2,1,0:T(8,128)}, f32[1,1,12,64,1280]{4,3,2,1,0:T(8,128)}, f32[1,1,12,64,1280]{4,3,2,1,0:T(8,128)}) fusion(f32[48,64,1280]{2,1,0:T(8,128)} %select_select_fusion), kind=kLoop, calls=%fused_computation.11 | loop fusion | bytes 31457280 | tf_op jit(solution)/shard_map/stack | solution.py:79
  106.1 6.3 pad_maximum_fusion
  112.3 345.5 %all_to_all.5 = f32[4,1,12,64,1280]{4,3,2,1,0:T(8,128)} all-to-all(f32[4,1,12,64,1280]{4,3,2,1,0:T(8,128)S(1)} %pad_maximum_fusion), channel_id=1, replica_groups=mesh['island'=2,'dp'=4,'tensor'=4] {'dp'}, dimensions={0} | all-to-all | bytes 31457280 | tf_op jit(solution)/shard_map/all_to_all | solution.py:79
  457.8 12.7 %copy.4 = f32[1,12,4,64,1280]{4,3,2,1,0:T(8,128)} copy(f32[1,12,4,64,1280]{4,3,1,0,2:T(8,128)} %bitcast.21) | data formatting | bytes 31457280 | tf_op jit(solution)/shard_map/reshape | solution.py:78
  470.6 22.1 %fusion.46 = f32[12,256,256]{2,1,0:T(8,128)} fusion(f32[12,256,1280]{2,1,0:T(8,128)} %bitcast.19), kind=kOutput, calls=%fused_computation.64 | convolution fusion | flops 12079595520 | bytes 18874368 | tf_op jit(solution)/shard_map/khc,kgc->khg/dot_general | solution.py:41
  492.8 86.2 %all-reduce.5.cloned.1.call-done = f32[12,256,256]{2,1,0:T(8,128)} async-done(((f32[12,256,256]{2,1,0:T(8,128)}), f32[12,256,256]{2,1,0:T(8,128)}) %all-reduce.5.cloned.1.call-update) | async-done | bytes 3145744 | tf_op jit(solution)/shard_map/psum | solution.py:42
  579.0 2.5 select_reduce_fusion
  581.5 0.3 copy-done
  581.8 3.4 fusion.20
  585.3 4.1 fusion.14
  589.4 3.8 fusion.13
  593.2 3.4 fusion.47
  596.7 4.5 fusion.8
  601.2 20.8 %fusion.5 = bf16[1,12,256,1280]{3,2,1,0:T(8,128)(2,1)} fusion(f32[12,256,256]{2,1,0:T(8,128)S(1)} %fusion.8, f32[12,256,1280]{2,1,0:T(8,128)} %bitcast.20, f32[12]{0:T(128)S(1)} %get-tuple-element.6), kind=kOutput, calls=%fused_computation.7 | convolution fusion | flops 12091392000 | bytes 26738736 | tf_op jit(solution)/shard_map/khg,kgc->khc/dot_general | solution.py:32
  (10 shorter events, 0.1 us)
Async XLA Ops:
  6.5 61.9 %all-reduce.3.cloned.1.call-start = ((), (), s32[]{:S(2)}) async-start(), calls=%async_computation.1 | async-start | bytes 31457280 | tf_op jit(solution)/shard_map/psum | solution.py:66
  6.5 0.8 copy-start.1
  7.3 571.7 %all-reduce.5.cloned.1.call-start = ((), (), s32[]{:S(2)}) async-start(), calls=%async_computation.2 | async-start | bytes 6291456 | tf_op jit(solution)/shard_map/psum | solution.py:42
  579.0 2.8 copy-start
Sparse Core Ops, SparseCore 0:
  9.8 58.5 all-reduce.2
  492.9 86.0 all-reduce.4
